TPU v7x, 32 devices: a whole 2x2x4 slice. The times are simulated.
32 devices in a mesh: dp: 8 (over z, y), tensor: 4 (over x, core).
Axes of the slice: x: 2, y: 2, z: 4, core: 2. Of those that a mesh axis runs over, the one named last changes fastest.
Arguments:
- tokens: bfloat16 [16384, 1536], P(('dp', 'tensor')), may hold values from -6 to 6
- segments: int32 [16384], P('dp'), may hold values from 0 to 3, as said below
- positions: int32 [16384], P('dp'), may hold values from 0 to 2044, as said below
- norm_attn: float32 [1536], replicated, may hold values from 0.1 to 1.9
- w_query: bfloat16 [1536, 1536], P(None, 'tensor'), may hold values from -0.15625 to 0.15625
- key_weight: bfloat16 [1536, 768], P(None, 'tensor'), may hold values from -0.15625 to 0.15625
- value_weight: bfloat16 [1536, 768], P(None, 'tensor'), may hold values from -0.15625 to 0.15625
- w_out: bfloat16 [1536, 1536], P('tensor'), may hold values from -1.5 to 1.5
- norm_mlp: float32 [1536], replicated, may hold values from 0.1 to 1.9
- w_gate: bfloat16 [1536, 4096], P(None, 'tensor'), may hold values from -0.15625 to 0.15625
- w_up: bfloat16 [1536, 4096], P(None, 'tensor'), may hold values from -0.15625 to 0.15625
- w_down: bfloat16 [4096, 1536], P('tensor'), may hold values from -0.09375 to 0.09375
- cotangent: bfloat16 [16384, 1536], P(('dp', 'tensor')), may hold values from -6 to 6
Outputs:
- output: bfloat16 [16384, 1536], P(('dp', 'tensor'))
- grad_tokens: float32 [16384, 1536], P(('dp', 'tensor'))
- grad_norm_attn: float32 [1536], replicated
- grad_w_query: float32 [1536, 1536], P(None, 'tensor')
- grad_w_key: float32 [1536, 768], P(None, 'tensor')
- grad_w_value: float32 [1536, 768], P(None, 'tensor')
- grad_w_out: float32 [1536, 1536], P('tensor')
- grad_norm_mlp: float32 [1536], replicated
- grad_w_gate: float32 [1536, 4096], P(None, 'tensor')
- grad_w_up: float32 [1536, 4096], P(None, 'tensor')
- grad_w_down: float32 [4096, 1536], P('tensor')
Inputs may be any that keep to these rules, and one draw needn't show every extreme that they name: `segments`: within each sequence of 2048 tokens the document numbers never fall, start at 0 and end at 3, each document one token or more. `positions`: each token's position within its document, 0 at the document's first token; the first sequence holds a document of 2045 tokens.
All inputs are finite; a program needn't handle non-finite values.
Results may differ from a plain program's by a relative error of at most 0.018.
Values may be sent and summed in bfloat16 or wider, within the bound.
A program may use at most 256 MiB of HBM per device.

v0:
```python
import math
import jax
import jax.numpy as jnp
from jax import lax
from jax.sharding import PartitionSpec as P

HEAD_SIZE = 96
epsilon = 1e-05
rope_base = 100000.0
masked_value = -1e30


def angle_tables(positions, width):
    middle = width // 2
    freq_steps = jnp.arange(middle, dtype=jnp.float32)
    inverse = jnp.exp(freq_steps * (-2.0 * math.log(rope_base) / width))
    angles = positions.astype(jnp.float32)[:, None] * inverse[None, :]
    return (jnp.cos(angles)[:, None, :], jnp.sin(angles)[:, None, :])


def apply_rotary(values, cosine_lookup, sine_lookup):
    middle = values.shape[-1] // 2
    front, second = (values[..., :middle], values[..., middle:])
    return jnp.concatenate(
        [
            front * cosine_lookup - second * sine_lookup,
            second * cosine_lookup + front * sine_lookup,
        ],
        axis=-1,
    )


def rotate_back(grads_in, cosine_lookup, sine_lookup):
    middle = grads_in.shape[-1] // 2
    front, second = (grads_in[..., :middle], grads_in[..., middle:])
    return jnp.concatenate(
        [
            front * cosine_lookup + second * sine_lookup,
            second * cosine_lookup - front * sine_lookup,
        ],
        axis=-1,
    )


def rms_inverse(values):
    return lax.rsqrt(jnp.mean(values * values, axis=-1, keepdims=True) + epsilon)


def norm_back(grad_normed, gain, unit_rows, inverse):
    scaled = grad_normed * gain
    return inverse * (scaled - unit_rows * jnp.mean(scaled * unit_rows, axis=-1, keepdims=True))


def contract_rows(left, right):
    return lax.dot_general(
        left, right, (((0,), (0,)), ((), ())), preferred_element_type=jnp.float32
    )


def contract_cols(left, right):
    return lax.dot_general(
        left, right, (((1,), (1,)), ((), ())), preferred_element_type=jnp.float32
    )


def block_scores(query_block, heads_of_key, allowed, score_scale):
    scores = (
        jnp.einsum("qgrd,kgd->grqk", query_block, heads_of_key, preferred_element_type=jnp.float32)
        * score_scale
    )
    return jnp.where(allowed[None, None], scores, masked_value)


def body(
    tokens,
    segments,
    positions,
    norm_attn,
    w_query,
    key_weight,
    value_weight,
    w_out,
    norm_mlp,
    w_gate,
    w_up,
    w_down,
    cotangent,
):
    sequence_length = segments.shape[0]
    q_heads = w_query.shape[1] // HEAD_SIZE
    kv_heads = key_weight.shape[1] // HEAD_SIZE
    head_repetitions = q_heads // kv_heads
    score_scale = 1.0 / math.sqrt(HEAD_SIZE)
    rows_per_block = min(512, sequence_length)
    block_total = sequence_length // rows_per_block
    cosine_lookup, sine_lookup = angle_tables(positions, HEAD_SIZE)
    indices = jnp.arange(sequence_length, dtype=jnp.int32)
    seg_blocks = segments.reshape(block_total, rows_per_block)
    index_blocks = indices.reshape(block_total, rows_per_block)
    inputs = tokens.astype(jnp.float32)
    inverse_one = rms_inverse(inputs)
    unit_one = inputs * inverse_one
    first_normalized = (unit_one * norm_attn).astype(jnp.bfloat16)
    attn_in = lax.all_gather(first_normalized, "tensor", axis=0, tiled=True)
    query_proj = jnp.dot(attn_in, w_query, preferred_element_type=jnp.float32).reshape(
        sequence_length, q_heads, HEAD_SIZE
    )
    key_proj = jnp.dot(attn_in, key_weight, preferred_element_type=jnp.float32).reshape(
        sequence_length, kv_heads, HEAD_SIZE
    )
    query_rows = apply_rotary(query_proj, cosine_lookup, sine_lookup).astype(jnp.bfloat16)
    heads_of_key = apply_rotary(key_proj, cosine_lookup, sine_lookup).astype(jnp.bfloat16)
    heads_of_value = (
        jnp.dot(attn_in, value_weight, preferred_element_type=jnp.float32)
        .astype(jnp.bfloat16)
        .reshape(sequence_length, kv_heads, HEAD_SIZE)
    )
    blocks_of_query = query_rows.reshape(
        block_total, rows_per_block, kv_heads, head_repetitions, HEAD_SIZE
    )

    def attend(member):
        query_block, rows_seg, rows_idx = member
        allowed = (rows_seg[:, None] == segments[None, :]) & (indices[None, :] <= rows_idx[:, None])
        scores = block_scores(query_block, heads_of_key, allowed, score_scale)
        row_peak = jnp.max(scores, axis=-1, keepdims=True)
        weights = jnp.exp(scores - row_peak)
        totals = jnp.sum(weights, axis=-1, keepdims=True)
        weights_low = (weights / totals).astype(jnp.bfloat16)
        mixed_heads = jnp.einsum(
            "grqk,kgd->qgrd", weights_low, heads_of_value, preferred_element_type=jnp.float32
        )
        return (mixed_heads.astype(jnp.bfloat16), row_peak[..., 0] + jnp.log(totals[..., 0]))

    attended, log_totals = lax.map(attend, (blocks_of_query, seg_blocks, index_blocks))
    attended = attended.reshape(sequence_length, q_heads * HEAD_SIZE)
    row_slice = attended
    attn_out = lax.psum_scatter(
        jnp.dot(row_slice, w_out, preferred_element_type=jnp.float32),
        "tensor",
        scatter_dimension=0,
        tiled=True,
    )
    hidden_one = inputs + attn_out
    inverse_two = rms_inverse(hidden_one)
    unit_two = hidden_one * inverse_two
    normed_two = (unit_two * norm_mlp).astype(jnp.bfloat16)
    mlp_in = lax.all_gather(normed_two, "tensor", axis=0, tiled=True)
    gate_proj = jnp.dot(mlp_in, w_gate, preferred_element_type=jnp.float32)
    up_proj = jnp.dot(mlp_in, w_up, preferred_element_type=jnp.float32)
    sigmoid_gate = jax.nn.sigmoid(gate_proj)
    activated = gate_proj * sigmoid_gate
    hidden = (activated * up_proj).astype(jnp.bfloat16)
    row_slice = hidden
    mlp_out = lax.psum_scatter(
        jnp.dot(row_slice, w_down, preferred_element_type=jnp.float32).astype(jnp.bfloat16),
        "tensor",
        scatter_dimension=0,
        tiled=True,
    ).astype(jnp.float32)
    output = (hidden_one + mlp_out).astype(jnp.bfloat16)
    grad_out = lax.all_gather(cotangent, "tensor", axis=0, tiled=True)
    grad_w_down = contract_rows(hidden, grad_out)
    grad_hidden = contract_cols(grad_out, w_down)
    grad_gate = (
        grad_hidden * up_proj * sigmoid_gate * (1.0 + gate_proj * (1.0 - sigmoid_gate))
    ).astype(jnp.bfloat16)
    grad_upper = (grad_hidden * activated).astype(jnp.bfloat16)
    grad_w_gate = contract_rows(mlp_in, grad_gate)
    grad_w_up = contract_rows(mlp_in, grad_upper)
    grad_normed_two = lax.psum_scatter(
        contract_cols(grad_gate, w_gate) + contract_cols(grad_upper, w_up),
        "tensor",
        scatter_dimension=0,
        tiled=True,
    )
    grad_norm_mlp = jnp.sum(grad_normed_two * unit_two, axis=0)
    grad_hidden_one = cotangent.astype(jnp.float32) + norm_back(
        grad_normed_two, norm_mlp, unit_two, inverse_two
    )
    grad_attn_rows = lax.all_gather(
        grad_hidden_one.astype(jnp.bfloat16), "tensor", axis=0, tiled=True
    )
    grad_w_out = contract_rows(attended, grad_attn_rows)
    grad_attended = contract_cols(grad_attn_rows, w_out).astype(jnp.bfloat16)
    grad_blocks = grad_attended.reshape(
        block_total, rows_per_block, kv_heads, head_repetitions, HEAD_SIZE
    )

    def attend_back(running, member):
        query_block, grad_block, rows_seg, rows_idx, log_block = member
        allowed = (rows_seg[:, None] == segments[None, :]) & (indices[None, :] <= rows_idx[:, None])
        scores = block_scores(query_block, heads_of_key, allowed, score_scale)
        weights = jnp.exp(scores - log_block[..., None])
        grad_weights = jnp.einsum(
            "qgrd,kgd->grqk", grad_block, heads_of_value, preferred_element_type=jnp.float32
        )
        inner_sum = jnp.sum(weights * grad_weights, axis=-1, keepdims=True)
        grad_scores = (weights * (grad_weights - inner_sum)).astype(jnp.bfloat16)
        grad_query = (
            jnp.einsum(
                "grqk,kgd->qgrd", grad_scores, heads_of_key, preferred_element_type=jnp.float32
            )
            * score_scale
        )
        grad_keys = (
            running[0]
            + jnp.einsum(
                "grqk,qgrd->kgd", grad_scores, query_block, preferred_element_type=jnp.float32
            )
            * score_scale
        )
        grad_values = running[1] + jnp.einsum(
            "grqk,qgrd->kgd",
            weights.astype(jnp.bfloat16),
            grad_block,
            preferred_element_type=jnp.float32,
        )
        return ((grad_keys, grad_values), grad_query)

    zero_state = jnp.zeros((sequence_length, kv_heads, HEAD_SIZE), jnp.float32)
    (grad_keys, grad_values), grad_queries = lax.scan(
        attend_back,
        (zero_state, zero_state),
        (blocks_of_query, grad_blocks, seg_blocks, index_blocks, log_totals),
    )
    grad_queries = grad_queries.reshape(sequence_length, q_heads, HEAD_SIZE)
    grad_q_proj = (
        rotate_back(grad_queries, cosine_lookup, sine_lookup)
        .reshape(sequence_length, q_heads * HEAD_SIZE)
        .astype(jnp.bfloat16)
    )
    grad_k_proj = (
        rotate_back(grad_keys, cosine_lookup, sine_lookup)
        .reshape(sequence_length, kv_heads * HEAD_SIZE)
        .astype(jnp.bfloat16)
    )
    grad_v_proj = grad_values.reshape(sequence_length, kv_heads * HEAD_SIZE).astype(jnp.bfloat16)
    grad_w_query = contract_rows(attn_in, grad_q_proj)
    grad_w_key = contract_rows(attn_in, grad_k_proj)
    grad_w_value = contract_rows(attn_in, grad_v_proj)
    grad_normed_one = lax.psum_scatter(
        (
            contract_cols(grad_q_proj, w_query)
            + contract_cols(grad_k_proj, key_weight)
            + contract_cols(grad_v_proj, value_weight)
        ).astype(jnp.bfloat16),
        "tensor",
        scatter_dimension=0,
        tiled=True,
    ).astype(jnp.float32)
    grad_norm_attn = jnp.sum(grad_normed_one * unit_one, axis=0)
    grad_tokens = grad_hidden_one + norm_back(grad_normed_one, norm_attn, unit_one, inverse_one)
    grad_norm_attn, grad_norm_mlp = lax.psum((grad_norm_attn, grad_norm_mlp), ("dp", "tensor"))
    grad_w_query, grad_w_key, grad_w_value, grad_w_out, grad_w_gate, grad_w_up, grad_w_down = (
        lax.psum(grad_w_query.astype(jnp.bfloat16), "dp").astype(jnp.float32),
        lax.psum(grad_w_key.astype(jnp.bfloat16), "dp").astype(jnp.float32),
        lax.psum(grad_w_value.astype(jnp.bfloat16), "dp").astype(jnp.float32),
        lax.psum(grad_w_out.astype(jnp.bfloat16), "dp").astype(jnp.float32),
        lax.psum(grad_w_gate.astype(jnp.bfloat16), "dp").astype(jnp.float32),
        lax.psum(grad_w_up.astype(jnp.bfloat16), "dp").astype(jnp.float32),
        lax.psum(grad_w_down.astype(jnp.bfloat16), "dp").astype(jnp.float32),
    )
    return (
        output,
        grad_tokens,
        grad_norm_attn,
        grad_w_query,
        grad_w_key,
        grad_w_value,
        grad_w_out,
        grad_norm_mlp,
        grad_w_gate,
        grad_w_up,
        grad_w_down,
    )


def solution(mesh):
    in_specs = (
        P(("dp", "tensor"), None),
        P("dp"),
        P("dp"),
        P(),
        P(None, "tensor"),
        P(None, "tensor"),
        P(None, "tensor"),
        P("tensor", None),
        P(),
        P(None, "tensor"),
        P(None, "tensor"),
        P("tensor", None),
        P(("dp", "tensor"), None),
    )
    out_specs = (
        P(("dp", "tensor"), None),
        P(("dp", "tensor"), None),
        P(),
        P(None, "tensor"),
        P(None, "tensor"),
        P(None, "tensor"),
        P("tensor", None),
        P(),
        P(None, "tensor"),
        P(None, "tensor"),
        P("tensor", None),
    )
    return jax.shard_map(body, mesh=mesh, in_specs=in_specs, out_specs=out_specs, check_vma=False)
```

profile of v0, /device:TPU:0, one launch (start us, length us, event | category | flops | bytes accessed | tf_op | source)
XLA Modules:
  0.0 1461.6 jit_solution(5925052065785356915)
XLA Ops:
  15.7 46.3 %all-gather.5.cloned.1.call-done = bf16[2048,1536]{1,0:T(8,128)(2,1)} async-done(((bf16[512,1536]{1,0:T(8,128)(2,1)}), bf16[2048,1536]{1,0:T(8,128)(2,1)}) %all-gather.5.cloned.1.call-update) | async-done | bytes 6291472 | tf_op jit(solution)/shard_map/all_gather | solution.py:104
  62.0 5.2 fusion.71
  84.0 5.9 convolution_convert_fusion.9
  89.8 66.6 %while.28 = (s32[]{:T(128)}, bf16[4,512,2,2,96]{1,4,3,2,0:T(8,128)(2,1)}, f32[4,2,2,512]{3,2,1,0:T(2,128)}, s32[4,512]{1,0:T(4,128)S(1)}, s32[2048]{0:T(1024)S(1...) while((s32[]{:T(128)}, ...), condition=%wide.region_4.5_spmd.clone, body=%wide.region_1.4_spmd.clone.sunk | while | flops 1664284672 | bytes 60117144 | solution.py:135
  91.2 4.7 bitcast_reduce_fusion.2
  96.0 4.4 fusion.143
  100.4 5.6 fusion.144
  107.8 4.7 bitcast_reduce_fusion.2
  112.6 4.4 fusion.143
  117.0 5.6 fusion.144
  124.4 4.7 bitcast_reduce_fusion.2
  129.2 4.4 fusion.143
  133.5 5.6 fusion.144
  141.0 4.7 bitcast_reduce_fusion.2
  145.7 4.4 fusion.143
  150.1 5.6 fusion.144
  160.8 6.4 fusion.72
  167.2 99.1 %reduce-scatter.5.cloned.1.call-done = f32[512,1536]{1,0:T(8,128)} async-done(((f32[2048,1536]{1,0:T(8,128)}), f32[512,1536]{1,0:T(8,128)}) %reduce-scatter.5.cloned.1.call-update) | async-done | bytes 3145744 | tf_op jit(solution)/shard_map/reduce_scatter | solution.py:138
  273.0 45.9 %all-gather.7.cloned.1.call-done = bf16[2048,1536]{1,0:T(8,128)(2,1)} async-done(((bf16[512,1536]{1,0:T(8,128)(2,1)}), bf16[2048,1536]{1,0:T(8,128)(2,1)}) %all-gather.7.cloned.1.call-update) | async-done | bytes 6291472 | tf_op jit(solution)/shard_map/all_gather | solution.py:148
  318.9 12.6 fusion.74
  331.5 8.8 fusion.73
  340.3 26.4 %all-gather.9.cloned.1.call-done = bf16[2048,1536]{1,0:T(8,128)(2,1)} async-done(((bf16[512,1536]{1,0:T(8,128)(2,1)}), bf16[2048,1536]{1,0:T(8,128)(2,1)}) %all-gather.9.cloned.1.call-update) | async-done | bytes 6291472 | tf_op jit(solution)/shard_map/all_gather | solution.py:162
  366.8 18.8 %multiply_convert_fusion = (bf16[2048,1024]{1,0:T(8,128)(2,1)}, bf16[2048,1024]{1,0:T(8,128)(2,1)}, bf16[2048,1024]{1,0:T(8,128)(2,1)}) fusion(f32[2048,1024]{1,0:T(8,128)} %fusion.73, f32[2048,1024]{1,0:T(8,128)} %fusion.74, bf16[2048,1536]{1,0:T(8,128)(2,1)} %all-gather.9.cloned.1.call-done, bf16[1024,1536]{1,0:T(8,128)(2,1)S(1)} %copy-done), kind=kOutput, calls=%fused_computation.69 | convolution fusion | flops 6473908224 | bytes 38797312 | tf_op jit(solution)/shard_map/dot_general | solution.py:61
  385.6 11.6 fusion.75
  397.2 12.9 convolution_add_fusion
  410.1 99.1 %reduce-scatter.9.cloned.1.call-done = f32[512,1536]{1,0:T(8,128)} async-done(((f32[2048,1536]{1,0:T(8,128)}), f32[512,1536]{1,0:T(8,128)}) %reduce-scatter.9.cloned.1.call-update) | async-done | bytes 3145744 | tf_op jit(solution)/shard_map/reduce_scatter | solution.py:171
  517.6 46.5 %all-gather.11.cloned.1.call-done = bf16[2048,1536]{1,0:T(8,128)(2,1)} async-done(((bf16[512,1536]{1,0:T(8,128)(2,1)}), bf16[2048,1536]{1,0:T(8,128)(2,1)}) %all-gather.11.cloned.1.call-update) | async-done | bytes 6291472 | tf_op jit(solution)/shard_map/all_gather | solution.py:181
  564.1 7.7 convolution_convert_fusion.6
  571.8 7.0 reshape.300
  578.7 6.0 copy.29
  584.7 274.0 %while.29 = (s32[]{:T(128)}, f32[2048,2,96]{0,2,1:T(8,128)}, f32[2048,2,96]{0,2,1:T(8,128)}, f32[4,512,2,2,96]{1,0,4,3,2:T(4,128)}, bf16[4,512,2,2,96]{1,4,3,2,0...) while((s32[]{:T(128)}, f32[2048,2,96]{0,2,1:T(8,128)}, ...), condition=%wide.region_12.13_spmd.clone, body=%wide.region_10.12_spmd.clone.sunk | while | flops 4094752768 | bytes 214511840 | solution.py:222
  590.7 5.8 copy-done.1
  596.5 7.1 fusion.158
  603.6 12.6 fusion.155
  616.3 12.2 fusion.156
  636.6 16.1 %dynamic_update_slice.22 = f32[4,512,2,2,96]{1,0,4,3,2:T(4,128)} dynamic-update-slice(f32[4,512,2,2,96]{1,0,4,3,2:T(4,128)} %get-tuple-element.503, f32[1,512,2,2,96]{1,0,4,3,2:T(1,128)} %copy.49, s32[]{:T(128)S(6)} %copy.66, s32[]{:T(128)} %constant.58.clone.1..sunk, s32[]{:T(128)} %constant.58.clone.1..sunk, s32[]{:T(128)} %constant.58.clone.1..sunk, s32[]{:T(128)} %constant.58.clone.1..sunk) | dynamic-update-slice | bytes 1572868 | tf_op jit(solution)/shard_map/while/body/jit(dynamic_update_index_in_dim)/dynamic_update_slice | solution.py:222
  658.2 5.8 copy-done.1
  664.0 7.7 fusion.158
  671.7 12.6 fusion.155
  684.3 12.2 fusion.156
  705.2 16.1 %dynamic_update_slice.22 = f32[4,512,2,2,96]{1,0,4,3,2:T(4,128)} dynamic-update-slice(f32[4,512,2,2,96]{1,0,4,3,2:T(4,128)} %get-tuple-element.503, f32[1,512,2,2,96]{1,0,4,3,2:T(1,128)} %copy.49, s32[]{:T(128)S(6)} %copy.66, s32[]{:T(128)} %constant.58.clone.1..sunk, s32[]{:T(128)} %constant.58.clone.1..sunk, s32[]{:T(128)} %constant.58.clone.1..sunk, s32[]{:T(128)} %constant.58.clone.1..sunk) | dynamic-update-slice | bytes 1572868 | tf_op jit(solution)/shard_map/while/body/jit(dynamic_update_index_in_dim)/dynamic_update_slice | solution.py:222
  726.9 5.8 copy-done.1
  732.7 7.7 fusion.158
  740.3 12.6 fusion.155
  753.0 12.2 fusion.156
  773.8 16.1 %dynamic_update_slice.22 = f32[4,512,2,2,96]{1,0,4,3,2:T(4,128)} dynamic-update-slice(f32[4,512,2,2,96]{1,0,4,3,2:T(4,128)} %get-tuple-element.503, f32[1,512,2,2,96]{1,0,4,3,2:T(1,128)} %copy.49, s32[]{:T(128)S(6)} %copy.66, s32[]{:T(128)} %constant.58.clone.1..sunk, s32[]{:T(128)} %constant.58.clone.1..sunk, s32[]{:T(128)} %constant.58.clone.1..sunk, s32[]{:T(128)} %constant.58.clone.1..sunk) | dynamic-update-slice | bytes 1572868 | tf_op jit(solution)/shard_map/while/body/jit(dynamic_update_index_in_dim)/dynamic_update_slice | solution.py:222
  795.5 5.8 copy-done.1
  801.3 7.7 fusion.158
  809.0 12.6 fusion.155
  821.6 12.2 fusion.156
  842.5 16.1 %dynamic_update_slice.22 = f32[4,512,2,2,96]{1,0,4,3,2:T(4,128)} dynamic-update-slice(f32[4,512,2,2,96]{1,0,4,3,2:T(4,128)} %get-tuple-element.503, f32[1,512,2,2,96]{1,0,4,3,2:T(1,128)} %copy.49, s32[]{:T(128)S(6)} %copy.66, s32[]{:T(128)} %constant.58.clone.1..sunk, s32[]{:T(128)} %constant.58.clone.1..sunk, s32[]{:T(128)} %constant.58.clone.1..sunk, s32[]{:T(128)} %constant.58.clone.1..sunk) | dynamic-update-slice | bytes 1572868 | tf_op jit(solution)/shard_map/while/body/jit(dynamic_update_index_in_dim)/dynamic_update_slice | solution.py:222
  858.7 5.3 reshape.293
  870.0 6.5 fusion.76
  876.6 6.4 fusion.77
  883.0 12.8 add_convert_fusion
  895.9 10.9 convolution_convert_fusion
  906.9 12.0 convolution_convert_fusion.2
  919.0 10.1 convolution_convert_fusion.3
  929.1 8.5 convolution_convert_fusion.1
  945.8 4.5 convolution_convert_fusion.5
  957.3 40.1 %all-reduce = (f32[1536]{0:T(1024)}, f32[1536]{0:T(1024)}) all-reduce(f32[1536]{0:T(1024)S(1)} %get-tuple-element.234, f32[1536]{0:T(1024)S(1)} %copy-done.41), channel_id=1, replica_groups=mesh['dp'=8,'tensor'=4] {'dp','tensor'}, use_global_device_ids=true, to_apply=%region_16.17 | all-reduce | flops 3072 | bytes 24576 | tf_op jit(solution)/shard_map/psum | solution.py:254
  997.4 19.3 %reduce-scatter.7.cloned.1.call-done = bf16[512,1536]{1,0:T(8,128)(2,1)} async-done(((bf16[2048,1536]{1,0:T(8,128)(2,1)}), bf16[512,1536]{1,0:T(8,128)(2,1)}) %reduce-scatter.7.cloned.1.call-update) | async-done | bytes 1572880 | tf_op jit(solution)/shard_map/reduce_scatter | solution.py:155
  1016.7 7.0 fusion.64
  1023.7 413.4 %all-reduce.4.cloned.1.call-done = (bf16[1536,384]{1,0:T(8,128)(2,1)}, bf16[1536,192]{0,1:T(8,128)(2,1)}, bf16[1536,192]{0,1:T(8,128)(2,1)}, bf16[384,1536]{1,0:...) async-done(((bf16[1536,384]{1,0:T(8,128)(2,1)}, bf16[1536,192]{0,1:T(8,128)(2,1)}, bf16[1536,192]{0,1:T(8,128)(2,1)}, ...) | async-done | bytes 12976144 | tf_op jit(solution)/shard_map/psum | solution.py:256
  (244 shorter events, 146.7 us)
Async XLA Ops:
  7.2 359.6 %copy-start = (bf16[1024,1536]{1,0:T(8,128)(2,1)S(1)}, bf16[1024,1536]{1,0:T(8,128)(2,1)}, u32[]{:S(2)}) copy-start(bf16[1024,1536]{1,0:T(8,128)(2,1)} %param.28) | copy-start | bytes 9437188
  7.2 5.7 copy-start.29
  7.2 5.7 copy-start.46
  7.2 54.8 %all-gather.5.cloned.1.call-start = ((), (), s32[]{:S(2)}) async-start(), calls=%async_computation.4 | async-start | bytes 7864320 | tf_op jit(solution)/shard_map/all_gather | solution.py:104
  12.8 253.6 %reduce-scatter.5.cloned.1.call-start = ((), (), s32[]{:S(2)}) async-start(), calls=%async_computation.5 | async-start | bytes 15728640 | tf_op jit(solution)/shard_map/reduce_scatter | solution.py:138
  15.7 55.7 %copy-start.7 = (f32[2048,48]{0,1:T(8,128)}, f32[2048,48]{0,1:T(8,128)S(1)}, u32[]{:S(2)}) copy-start(f32[2048,48]{0,1:T(8,128)S(1)} %get-tuple-element.310) | copy-start | bytes 1179652
  62.0 5.2 copy-start.9
  62.0 6.4 copy-start.47
  79.1 4.0 copy-start.23
  79.1 4.0 copy-start.24
  84.0 5.9 copy-start.37
  96.0 4.4 copy-start.6
  112.5 4.4 copy-start.6
  129.1 4.4 copy-start.6
  145.7 4.4 copy-start.6
  156.4 4.4 copy-start.26
  167.2 103.7 %copy-start.35 = (f32[1536]{0:T(1024)S(1)}, f32[1536]{0:T(1024)}, u32[]{:S(2)}) copy-start(f32[1536]{0:T(1024)} %param.25) | copy-start | bytes 18436
  167.2 151.7 %all-gather.7.cloned.1.call-start = ((), (), s32[]{:S(2)}) async-start(), calls=%async_computation.6 | async-start | bytes 7864320 | tf_op jit(solution)/shard_map/all_gather | solution.py:148
  269.2 244.4 %copy-start.39 = (f32[512]{0:T(512)}, f32[512]{0:T(512)S(1)}, u32[]{:S(2)}) copy-start(f32[512]{0:T(512)S(1)} %add_rsqrt_fusion) | copy-start | bytes 6148
  272.4 94.4 %all-gather.9.cloned.1.call-start = ((), (), s32[]{:S(2)}) async-start(), calls=%async_computation.8 | async-start | bytes 7864320 | tf_op jit(solution)/shard_map/all_gather | solution.py:162
  273.0 236.3 %reduce-scatter.9.cloned.1.call-start = ((), (), s32[]{:S(2)}) async-start(), calls=%async_computation.9 | async-start | bytes 15728640 | tf_op jit(solution)/shard_map/reduce_scatter | solution.py:171
  318.9 12.6 copy-start.48
  318.9 12.6 copy-start.49
  366.8 18.8 %copy-start.50 = (bf16[1536,1024]{1,0:T(8,128)(2,1)S(1)}, bf16[1536,1024]{1,0:T(8,128)(2,1)}, u32[]{:S(2)}) copy-start(bf16[1536,1024]{1,0:T(8,128)(2,1)} %param.26) | copy-start | bytes 9437188
  385.5 11.6 copy-start.51
  385.5 11.6 copy-start.53
  410.1 154.0 %all-gather.11.cloned.1.call-start = ((), (), s32[]{:S(2)}) async-start(), calls=%async_computation.10 | async-start | bytes 7864320 | tf_op jit(solution)/shard_map/all_gather | solution.py:181
  509.3 4.4 copy-start.4
  509.3 4.7 copy-start.5
  517.5 436.8 %reduce-scatter.11.cloned.1.call-start = ((), (), s32[]{:S(2)}) async-start(), calls=%async_computation.11 | async-start | bytes 7864320 | tf_op jit(solution)/shard_map/reduce_scatter | solution.py:242
  590.7 5.8 copy-start.1
  616.2 12.2 copy-start.2
  658.2 5.8 copy-start.1
  684.3 12.2 copy-start.2
  726.9 5.8 copy-start.1
  753.0 12.2 copy-start.2
  795.5 5.8 copy-start.1
  821.6 12.2 copy-start.2
  858.7 5.3 copy-start.8
  864.0 4.2 copy-start.22
  868.4 14.7 %copy-start.20 = (bf16[2048,2,96]{0,2,1:T(8,128)(2,1)}, bf16[2048,2,96]{0,2,1:T(8,128)(2,1)S(1)}, u32[]{:S(2)}) copy-start(bf16[2048,2,96]{0,2,1:T(8,128)(2,1)S(1)} %convert_element_type.138) | copy-start | bytes 2359300
  868.5 8.0 copy-start.13
  870.0 6.6 copy-start.32
  876.6 6.4 copy-start.15
  876.6 6.4 copy-start.34
  895.8 120.9 %reduce-scatter.7.cloned.1.call-start = ((), (), s32[]{:S(2)}) async-start(), calls=%async_computation.7 | async-start | bytes 7864320 | tf_op jit(solution)/shard_map/reduce_scatter | solution.py:155
  906.8 530.3 %all-reduce.4.cloned.1.call-start = ((), (), s32[]{:S(2)}) async-start(), calls=%async_computation.12 | async-start | bytes 25952256 | tf_op jit(solution)/shard_map/psum | solution.py:256
  906.9 12.1 copy-start.52
  906.9 22.2 %slice-start.2 = ((s8[6291456]{0:T(1024)(128)(4,1)}), s8[4194304]{0:T(1024)(128)(4,1)S(1)}, s32[]{:S(2)}) async-start(s8[6291456]{0:T(1024)(128)(4,1)} %bitcast.262), calls=%async_computation.15 | async-start | bytes 8388608
  918.9 10.2 slice-start.3
  918.9 10.2 copy-start.54
  918.9 18.7 %slice-start = ((s8[6291456]{0:T(1024)(128)(4,1)}), s8[4194304]{0:T(1024)(128)(4,1)S(1)}, s32[]{:S(2)}) async-start(s8[6291456]{0:T(1024)(128)(4,1)} %bitcast.260), calls=%async_computation.13 | async-start | bytes 8388608
  929.1 8.6 copy-start.16
  929.1 8.6 slice-start.1
  937.7 4.4 slice-start.4
  950.3 4.0 copy-start.38
  950.3 4.0 copy-start.43
  950.4 6.9 copy-start.41
  950.4 66.3 %copy-start.36 = (f32[1536]{0:T(1024)S(1)}, f32[1536]{0:T(1024)}, u32[]{:S(2)}) copy-start(f32[1536]{0:T(1024)} %param.25) | copy-start | bytes 18436
  950.4 66.3 %copy-start.40 = (f32[512]{0:T(512)S(1)}, f32[512]{0:T(512)}, u32[]{:S(2)}) copy-start(f32[512]{0:T(512)} %copy-done.39) | copy-start | bytes 6148
  950.4 66.3 %copy-start.45 = (f32[512]{0:T(512)S(1)}, f32[512]{0:T(512)}, u32[]{:S(2)}) copy-start(f32[512]{0:T(512)} %copy-done.44) | copy-start | bytes 6148
  1437.1 4.1 copy-start.30
  1437.1 5.3 copy-start.25
  1440.1 4.0 copy-start.19
  (15 other events, 35.5 us)
Sparse Core Ops, SparseCore 0:
  12.9 49.0 all-gather.4
  167.3 99.0 reduce-scatter.4
  272.5 46.3 all-gather.6
  320.3 46.3 all-gather.8
  410.2 99.0 reduce-scatter.8
  517.7 46.3 all-gather.10
  895.9 58.3 reduce-scatter.10
  957.6 59.0 reduce-scatter.6
  1023.5 413.5 all-reduce.3
where the time goes:
time: 1470 us; the launch traced here: 1460 us
  waiting for transfers between devices  801 us (54%)
  matrix products  336 us (23%)
  other arithmetic  136 us (9%)
  local copies, waits for them, and re-layouts  132 us (9%)
  blocking collectives  40.1 us (3%)
  between operations  14.9 us (1%)
    psum x1, waiting for transfers between devices, body(): lax.psum(grad_w_query.astype(jnp.bfloat16), 'dp').astype(jnp.float32)  413 us
    reduce_scatter x1, waiting for transfers between devices, body(): lax.psum_scatter(contract_cols(grad_gate, w_gate) + contract_cols(grad_up...  99.1 us
    reduce_scatter x1, waiting for transfers between devices, body(): lax.psum_scatter(jnp.dot(row_slice, w_out, preferred_element_type=jnp.flo...  99.1 us
    dot_general x7, matrix products, contract_cols(): lax.dot_general(left, right, (((1,), (1,)), ((), ())), preferred_element_...  76.6 us
    dynamic_update_slice x8, local copies, waits for them, and re-layouts, body(): lax.scan(attend_back, (zero_state, zero_state), (blocks_of_query, grad_bl...  71.2 us
    dot_general x4, matrix products, attend_back(): jnp.einsum('qgrd,kgd->grqk', grad_block, heads_of_value, preferred_elemen...  50.6 us
    convert_element_type x4, other arithmetic, attend_back(): grad_scores = (weights * (grad_weights - inner_sum)).astype(jnp.bfloat16)  48.7 us
    all_gather x1, waiting for transfers between devices, body(): lax.all_gather(grad_hidden_one.astype(jnp.bfloat16), 'tensor', axis=0, ti...  46.5 us
  transfers between devices with their start and end apart: 9, of which 9 were waited for; matrix products, arithmetic and copies ran while one was open for 6% of the time, Pallas kernels for 0%

commit v1 on v0

--- a/solution.py
+++ b/solution.py
@@ -101,7 +101,14 @@
     inverse_one = rms_inverse(inputs)
     unit_one = inputs * inverse_one
     first_normalized = (unit_one * norm_attn).astype(jnp.bfloat16)
-    attn_in = lax.all_gather(first_normalized, "tensor", axis=0, tiled=True)
+    ring = [first_normalized]
+    for hop in range(3):
+        ring.append(lax.ppermute(ring[-1], "tensor", [(dev, (dev + 1) % 4) for dev in range(4)]))
+    attn_in = jnp.roll(
+        jnp.concatenate(ring[::-1], axis=0),
+        (lax.axis_index("tensor") + 1) * ring[0].shape[0],
+        axis=0,
+    )
     query_proj = jnp.dot(attn_in, w_query, preferred_element_type=jnp.float32).reshape(
         sequence_length, q_heads, HEAD_SIZE
     )

time: 1470 us -> 1490 us (1.014)
    ppermute x0 -> x3, waiting for transfers between devices: none -> 58 us  [body(): lax.ppermute(ring[-1], 'tensor', [(dev, (dev + 1) % 4) for dev in range(4)])]
    all_gather x1 -> x0, waiting for transfers between devices: 46.3 us -> none  [body(): attn_in = lax.all_gather(first_normalized, 'tensor', axis=0, tiled=True)]
  transfers between devices with their start and end apart: 9 -> 11, of which waited for: 9 -> 11; matrix products, arithmetic and copies ran while one was open for 6% -> 6% of each run, Pallas kernels for 0% -> 0%
where the time goes in v1:
time: 1490 us; the launch traced here: 1480 us
  waiting for transfers between devices  814 us (55%)
  matrix products  332 us (22%)
  local copies, waits for them, and re-layouts  145 us (10%)
  other arithmetic  135 us (9%)
  blocking collectives  40.1 us (3%)
  between operations  15.3 us (1%)
    psum x1, waiting for transfers between devices, body(): lax.psum(grad_w_query.astype(jnp.bfloat16), 'dp').astype(jnp.float32)  413 us
    reduce_scatter x1, waiting for transfers between devices, body(): lax.psum_scatter(jnp.dot(row_slice, w_out, preferred_element_type=jnp.flo...  101 us
    reduce_scatter x1, waiting for transfers between devices, body(): lax.psum_scatter(contract_cols(grad_gate, w_gate) + contract_cols(grad_up...  99.1 us
    dot_general x7, matrix products, contract_cols(): lax.dot_general(left, right, (((1,), (1,)), ((), ())), preferred_element_...  76.9 us
    dynamic_update_slice x8, local copies, waits for them, and re-layouts, body(): lax.scan(attend_back, (zero_state, zero_state), (blocks_of_query, grad_bl...  71.2 us
    ppermute x3, waiting for transfers between devices, body(): lax.ppermute(ring[-1], 'tensor', [(dev, (dev + 1) % 4) for dev in range(4)])  58 us
    dot_general x4, matrix products, attend_back(): jnp.einsum('qgrd,kgd->grqk', grad_block, heads_of_value, preferred_elemen...  50.6 us
    convert_element_type x4, other arithmetic, attend_back(): grad_scores = (weights * (grad_weights - inner_sum)).astype(jnp.bfloat16)  48.7 us
  transfers between devices with their start and end apart: 11, of which 11 were waited for; matrix products, arithmetic and copies ran while one was open for 6% of the time, Pallas kernels for 0%

profile of v1, /device:TPU:0, one launch (start us, length us, event | category | flops | bytes accessed | tf_op | source)
XLA Modules:
  0.0 1482.9 jit_solution(6523914538570943360)
XLA Ops:
  11.6 20.0 %collective-permute-done = bf16[512,1536]{1,0:T(8,128)(2,1)S(1)} collective-permute-done((bf16[512,1536]{1,0:T(8,128)(2,1)S(1)}, bf16[512,1536]{1,0:T(8,128)(2,1)S(1)}, u32[]{:S(2)}, u32[]{:S(2)}) %collective-permute-start) | collective-permute-done | bytes 1572896 | tf_op jit(solution)/shard_map/ppermute | solution.py:106
  32.7 19.9 %collective-permute-done.1 = bf16[512,1536]{1,0:T(8,128)(2,1)} collective-permute-done((bf16[512,1536]{1,0:T(8,128)(2,1)S(1)}, bf16[512,1536]{1,0:T(8,128)(2,1)}, u32[]{:S(2)}, u32[]{:S(2)}) %collective-permute-start.1) | collective-permute-done | bytes 1572896 | tf_op jit(solution)/shard_map/ppermute | solution.py:106
  54.8 18.0 %collective-permute-done.2 = bf16[512,1536]{1,0:T(8,128)(2,1)} collective-permute-done((bf16[512,1536]{1,0:T(8,128)(2,1)}, bf16[512,1536]{1,0:T(8,128)(2,1)}, u32[]{:S(2)}, u32[]{:S(2)}) %collective-permute-start.2) | collective-permute-done | bytes 1572896 | tf_op jit(solution)/shard_map/ppermute | solution.py:106
  103.1 69.1 %while.28 = (s32[]{:T(128)}, bf16[4,512,2,2,96]{1,4,3,2,0:T(8,128)(2,1)}, f32[4,2,2,512]{3,2,1,0:T(2,128)}, s32[4,512]{1,0:T(4,128)S(1)}, s32[2048]{0:T(1024)S(1...) while((s32[]{:T(128)}, ...), condition=%wide.region_4.5_spmd.clone, body=%wide.region_1.4_spmd.clone.sunk | while | flops 1664284672 | bytes 60117144 | solution.py:142
  105.0 4.7 bitcast_reduce_fusion.2
  109.7 4.4 fusion.161
  114.1 5.6 fusion.162
  122.3 4.7 bitcast_reduce_fusion.2
  127.0 4.4 fusion.161
  131.4 5.6 fusion.162
  139.5 4.7 bitcast_reduce_fusion.2
  144.3 4.4 fusion.161
  148.7 5.6 fusion.162
  156.8 4.7 bitcast_reduce_fusion.2
  161.5 4.4 fusion.161
  165.9 5.6 fusion.162
  176.5 6.4 fusion.96
  183.0 101.2 %reduce-scatter.5.cloned.1.call-done = f32[512,1536]{1,0:T(8,128)} async-done(((f32[2048,1536]{1,0:T(8,128)}), f32[512,1536]{1,0:T(8,128)}) %reduce-scatter.5.cloned.1.call-update) | async-done | bytes 3145744 | tf_op jit(solution)/shard_map/reduce_scatter | solution.py:145
  291.0 45.8 %all-gather.4.cloned.1.call-done = bf16[2048,1536]{1,0:T(8,128)(2,1)} async-done(((bf16[512,1536]{1,0:T(8,128)(2,1)}), bf16[2048,1536]{1,0:T(8,128)(2,1)}) %all-gather.4.cloned.1.call-update) | async-done | bytes 6291472 | tf_op jit(solution)/shard_map/all_gather | solution.py:155
  336.8 12.5 fusion.98
  349.3 8.9 fusion.97
  358.2 26.6 %all-gather.6.cloned.1.call-done = bf16[2048,1536]{1,0:T(8,128)(2,1)} async-done(((bf16[512,1536]{1,0:T(8,128)(2,1)}), bf16[2048,1536]{1,0:T(8,128)(2,1)}) %all-gather.6.cloned.1.call-update) | async-done | bytes 6291472 | tf_op jit(solution)/shard_map/all_gather | solution.py:169
  384.8 18.9 %multiply_convert_fusion = (bf16[2048,1024]{1,0:T(8,128)(2,1)}, bf16[2048,1024]{1,0:T(8,128)(2,1)}, bf16[2048,1024]{1,0:T(8,128)(2,1)}) fusion(f32[2048,1024]{1,0:T(8,128)} %fusion.97, f32[2048,1024]{1,0:T(8,128)} %fusion.98, bf16[2048,1536]{1,0:T(8,128)(2,1)} %all-gather.6.cloned.1.call-done, bf16[1024,1536]{1,0:T(8,128)(2,1)S(1)} %copy-done), kind=kOutput, calls=%fused_computation.69 | convolution fusion | flops 6473908224 | bytes 38797312 | tf_op jit(solution)/shard_map/dot_general | solution.py:61
  403.7 11.8 fusion.99
  415.5 12.9 convolution_add_fusion
  428.4 99.1 %reduce-scatter.9.cloned.1.call-done = f32[512,1536]{1,0:T(8,128)} async-done(((f32[2048,1536]{1,0:T(8,128)}), f32[512,1536]{1,0:T(8,128)}) %reduce-scatter.9.cloned.1.call-update) | async-done | bytes 3145744 | tf_op jit(solution)/shard_map/reduce_scatter | solution.py:178
  535.9 46.5 %all-gather.8.cloned.1.call-done = bf16[2048,1536]{1,0:T(8,128)(2,1)} async-done(((bf16[512,1536]{1,0:T(8,128)(2,1)}), bf16[2048,1536]{1,0:T(8,128)(2,1)}) %all-gather.8.cloned.1.call-update) | async-done | bytes 6291472 | tf_op jit(solution)/shard_map/all_gather | solution.py:188
  582.4 7.7 convolution_convert_fusion.6
  590.1 7.0 reshape.300
  597.1 6.0 copy.29
  603.0 276.7 %while.29 = (s32[]{:T(128)}, f32[2048,2,96]{0,2,1:T(8,128)}, f32[2048,2,96]{0,2,1:T(8,128)}, f32[4,512,2,2,96]{1,0,4,3,2:T(4,128)}, bf16[4,512,2,2,96]{1,4,3,2,0...) while((s32[]{:T(128)}, f32[2048,2,96]{0,2,1:T(8,128)}, ...), condition=%wide.region_12.13_spmd.clone, body=%wide.region_10.12_spmd.clone.sunk | while | flops 4094752768 | bytes 214511840 | solution.py:229
  609.7 5.8 copy-done.1
  615.5 7.1 fusion.176
  622.6 12.7 fusion.173
  635.3 12.2 fusion.174
  655.6 16.1 %dynamic_update_slice.22 = f32[4,512,2,2,96]{1,0,4,3,2:T(4,128)} dynamic-update-slice(f32[4,512,2,2,96]{1,0,4,3,2:T(4,128)} %get-tuple-element.503, f32[1,512,2,2,96]{1,0,4,3,2:T(1,128)} %copy.49, s32[]{:T(128)S(6)} %copy.73, s32[]{:T(128)} %constant.81.clone.1..sunk, s32[]{:T(128)} %constant.81.clone.1..sunk, s32[]{:T(128)} %constant.81.clone.1..sunk, s32[]{:T(128)} %constant.81.clone.1..sunk) | dynamic-update-slice | bytes 1572868 | tf_op jit(solution)/shard_map/while/body/jit(dynamic_update_index_in_dim)/dynamic_update_slice | solution.py:229
  677.9 5.8 copy-done.1
  683.7 7.7 fusion.176
  691.4 12.7 fusion.173
  704.0 12.2 fusion.174
  724.9 16.1 %dynamic_update_slice.22 = f32[4,512,2,2,96]{1,0,4,3,2:T(4,128)} dynamic-update-slice(f32[4,512,2,2,96]{1,0,4,3,2:T(4,128)} %get-tuple-element.503, f32[1,512,2,2,96]{1,0,4,3,2:T(1,128)} %copy.49, s32[]{:T(128)S(6)} %copy.73, s32[]{:T(128)} %constant.81.clone.1..sunk, s32[]{:T(128)} %constant.81.clone.1..sunk, s32[]{:T(128)} %constant.81.clone.1..sunk, s32[]{:T(128)} %constant.81.clone.1..sunk) | dynamic-update-slice | bytes 1572868 | tf_op jit(solution)/shard_map/while/body/jit(dynamic_update_index_in_dim)/dynamic_update_slice | solution.py:229
  747.2 5.8 copy-done.1
  753.0 7.7 fusion.176
  760.7 12.7 fusion.173
  773.3 12.2 fusion.174
  794.2 16.1 %dynamic_update_slice.22 = f32[4,512,2,2,96]{1,0,4,3,2:T(4,128)} dynamic-update-slice(f32[4,512,2,2,96]{1,0,4,3,2:T(4,128)} %get-tuple-element.503, f32[1,512,2,2,96]{1,0,4,3,2:T(1,128)} %copy.49, s32[]{:T(128)S(6)} %copy.73, s32[]{:T(128)} %constant.81.clone.1..sunk, s32[]{:T(128)} %constant.81.clone.1..sunk, s32[]{:T(128)} %constant.81.clone.1..sunk, s32[]{:T(128)} %constant.81.clone.1..sunk) | dynamic-update-slice | bytes 1572868 | tf_op jit(solution)/shard_map/while/body/jit(dynamic_update_index_in_dim)/dynamic_update_slice | solution.py:229
  816.6 5.8 copy-done.1
  822.3 7.7 fusion.176
  830.0 12.7 fusion.173
  842.6 12.2 fusion.174
  863.5 16.1 %dynamic_update_slice.22 = f32[4,512,2,2,96]{1,0,4,3,2:T(4,128)} dynamic-update-slice(f32[4,512,2,2,96]{1,0,4,3,2:T(4,128)} %get-tuple-element.503, f32[1,512,2,2,96]{1,0,4,3,2:T(1,128)} %copy.49, s32[]{:T(128)S(6)} %copy.73, s32[]{:T(128)} %constant.81.clone.1..sunk, s32[]{:T(128)} %constant.81.clone.1..sunk, s32[]{:T(128)} %constant.81.clone.1..sunk, s32[]{:T(128)} %constant.81.clone.1..sunk) | dynamic-update-slice | bytes 1572868 | tf_op jit(solution)/shard_map/while/body/jit(dynamic_update_index_in_dim)/dynamic_update_slice | solution.py:229
  879.8 5.3 reshape.293
  891.1 6.5 fusion.100
  897.6 6.4 fusion.101
  904.1 12.8 add_convert_fusion
  916.9 10.9 convolution_convert_fusion
  927.9 12.0 convolution_convert_fusion.2
  940.0 10.2 convolution_convert_fusion.3
  950.3 8.6 convolution_convert_fusion.1
  963.5 4.6 convolution_convert_fusion.5
  978.3 40.1 %all-reduce = (f32[1536]{0:T(1024)}, f32[1536]{0:T(1024)}) all-reduce(f32[1536]{0:T(1024)S(1)} %get-tuple-element.234, f32[1536]{0:T(1024)S(1)} %copy-done.47), channel_id=1, replica_groups=mesh['dp'=8,'tensor'=4] {'dp','tensor'}, use_global_device_ids=true, to_apply=%region_16.17 | all-reduce | flops 3072 | bytes 24576 | tf_op jit(solution)/shard_map/psum | solution.py:261
  1018.4 19.4 %reduce-scatter.7.cloned.1.call-done = bf16[512,1536]{1,0:T(8,128)(2,1)} async-done(((bf16[2048,1536]{1,0:T(8,128)(2,1)}), bf16[512,1536]{1,0:T(8,128)(2,1)}) %reduce-scatter.7.cloned.1.call-update) | async-done | bytes 1572880 | tf_op jit(solution)/shard_map/reduce_scatter | solution.py:162
  1037.7 7.0 fusion.64
  1044.7 413.4 %all-reduce.4.cloned.1.call-done = (bf16[1536,384]{1,0:T(8,128)(2,1)}, bf16[1536,192]{0,1:T(8,128)(2,1)}, bf16[1536,192]{0,1:T(8,128)(2,1)}, bf16[384,1536]{1,0:...) async-done(((bf16[1536,384]{1,0:T(8,128)(2,1)}, bf16[1536,192]{0,1:T(8,128)(2,1)}, bf16[1536,192]{0,1:T(8,128)(2,1)}, ...) | async-done | bytes 12976144 | tf_op jit(solution)/shard_map/psum | solution.py:263
  (263 shorter events, 164.5 us)
Async XLA Ops:
  7.2 377.6 %copy-start = (bf16[1024,1536]{1,0:T(8,128)(2,1)S(1)}, bf16[1024,1536]{1,0:T(8,128)(2,1)}, u32[]{:S(2)}) copy-start(bf16[1024,1536]{1,0:T(8,128)(2,1)} %param.28) | copy-start | bytes 9437188
  7.2 45.5 %copy-start.31 = (s32[2048]{0:T(1024)S(1)}, s32[2048]{0:T(1024)}, u32[]{:S(2)}) copy-start(s32[2048]{0:T(1024)} %param.18) | copy-start | bytes 24580
  7.2 45.5 %copy-start.50 = (s32[2048]{0:T(1024)S(1)}, s32[2048]{0:T(1024)}, u32[]{:S(2)}) copy-start(s32[2048]{0:T(1024)} %param.19) | copy-start | bytes 24580
  7.2 277.0 %reduce-scatter.5.cloned.1.call-start = ((), (), s32[]{:S(2)}) async-start(), calls=%async_computation.4 | async-start | bytes 15728640 | tf_op jit(solution)/shard_map/reduce_scatter | solution.py:145
  9.2 70.6 %copy-start.43 = (f32[512]{0:T(512)}, f32[512]{0:T(512)S(1)}, u32[]{:S(2)}) copy-start(f32[512]{0:T(512)S(1)} %add_rsqrt_fusion.1) | copy-start | bytes 6148
  11.1 20.5 %collective-permute-start = (bf16[512,1536]{1,0:T(8,128)(2,1)S(1)}, bf16[512,1536]{1,0:T(8,128)(2,1)S(1)}, u32[]{:S(2)}, u32[]{:S(2)}) collective-permute-start(bf16[512,1536]{1,0:T(8,128)(2,1)S(1)} %fusion.65), channel_id=1, source_target_pairs={{0,1},{1,2},{2,3},{3,0},{4,5},{5,6},{6,7},{7,4},{8,9},{9,10},{10,1... | collective-permute-start | bytes 4718600 | tf_op jit(solution)/shard_map/ppermute | solution.py:106
  32.7 19.9 %collective-permute-start.1 = (bf16[512,1536]{1,0:T(8,128)(2,1)S(1)}, bf16[512,1536]{1,0:T(8,128)(2,1)}, u32[]{:S(2)}, u32[]{:S(2)}) collective-permute-start(bf16[512,1536]{1,0:T(8,128)(2,1)S(1)} %collective-permute-done), channel_id=1, source_target_pairs={{0,1},{1,2},{2,3},{3,0},{4,5},{5,6},{6,7},{7,4},{8,9},{9,10},{10,1... | collective-permute-start | bytes 4718600 | tf_op jit(solution)/shard_map/ppermute | solution.py:106
  52.7 20.2 %collective-permute-start.2 = (bf16[512,1536]{1,0:T(8,128)(2,1)}, bf16[512,1536]{1,0:T(8,128)(2,1)}, u32[]{:S(2)}, u32[]{:S(2)}) collective-permute-start(bf16[512,1536]{1,0:T(8,128)(2,1)} %collective-permute-done.1), channel_id=1, source_target_pairs={{0,1},{1,2},{2,3},{3,0},{4,5},{5,6},{6,7},{7,4},{8,9},{9,10},{10,1... | collective-permute-start | bytes 4718600 | tf_op jit(solution)/shard_map/ppermute | solution.py:106
  54.8 35.6 %copy-start.8 = (f32[2048,48]{0,1:T(8,128)}, f32[2048,48]{0,1:T(8,128)S(1)}, u32[]{:S(2)}) copy-start(f32[2048,48]{0,1:T(8,128)S(1)} %get-tuple-element.310) | copy-start | bytes 1179652
  54.8 35.6 %copy-start.10 = (f32[2048,48]{0,1:T(8,128)}, f32[2048,48]{0,1:T(8,128)S(1)}, u32[]{:S(2)}) copy-start(f32[2048,48]{0,1:T(8,128)S(1)} %get-tuple-element.311) | copy-start | bytes 1179652
  54.8 21.2 %copy-start.15 = (bf16[512,1536]{1,0:T(8,128)(2,1)S(1)}, bf16[512,1536]{1,0:T(8,128)(2,1)}, u32[]{:S(2)}) copy-start(bf16[512,1536]{1,0:T(8,128)(2,1)} %copy-done.14) | copy-start | bytes 4718596
  80.8 5.9 copy-start.40
  109.7 4.4 copy-start.7
  127.0 4.4 copy-start.7
  144.3 4.4 copy-start.7
  161.5 4.4 copy-start.7
  172.2 4.3 copy-start.28
  183.0 105.8 %copy-start.41 = (f32[1536]{0:T(1024)S(1)}, f32[1536]{0:T(1024)}, u32[]{:S(2)}) copy-start(f32[1536]{0:T(1024)} %param.25) | copy-start | bytes 18436
  183.0 153.8 %all-gather.4.cloned.1.call-start = ((), (), s32[]{:S(2)}) async-start(), calls=%async_computation.5 | async-start | bytes 7864320 | tf_op jit(solution)/shard_map/all_gather | solution.py:155
  287.1 244.8 %copy-start.45 = (f32[512]{0:T(512)}, f32[512]{0:T(512)S(1)}, u32[]{:S(2)}) copy-start(f32[512]{0:T(512)S(1)} %add_rsqrt_fusion) | copy-start | bytes 6148
  290.2 94.5 %all-gather.6.cloned.1.call-start = ((), (), s32[]{:S(2)}) async-start(), calls=%async_computation.7 | async-start | bytes 7864320 | tf_op jit(solution)/shard_map/all_gather | solution.py:169
  291.0 236.6 %reduce-scatter.9.cloned.1.call-start = ((), (), s32[]{:S(2)}) async-start(), calls=%async_computation.8 | async-start | bytes 15728640 | tf_op jit(solution)/shard_map/reduce_scatter | solution.py:178
  336.8 12.6 copy-start.51
  336.8 12.6 copy-start.52
  384.8 18.9 %copy-start.53 = (bf16[1536,1024]{1,0:T(8,128)(2,1)S(1)}, bf16[1536,1024]{1,0:T(8,128)(2,1)}, u32[]{:S(2)}) copy-start(bf16[1536,1024]{1,0:T(8,128)(2,1)} %param.26) | copy-start | bytes 9437188
  403.7 11.8 copy-start.54
  403.7 11.8 copy-start.56
  428.4 154.0 %all-gather.8.cloned.1.call-start = ((), (), s32[]{:S(2)}) async-start(), calls=%async_computation.9 | async-start | bytes 7864320 | tf_op jit(solution)/shard_map/all_gather | solution.py:188
  527.6 4.4 copy-start.4
  527.6 4.7 copy-start.6
  535.8 439.5 %reduce-scatter.11.cloned.1.call-start = ((), (), s32[]{:S(2)}) async-start(), calls=%async_computation.10 | async-start | bytes 7864320 | tf_op jit(solution)/shard_map/reduce_scatter | solution.py:249
  609.7 5.8 copy-start.1
  635.3 12.2 copy-start.2
  677.9 5.8 copy-start.1
  704.0 12.2 copy-start.2
  747.2 5.8 copy-start.1
  773.3 12.2 copy-start.2
  816.5 5.8 copy-start.1
  842.6 12.2 copy-start.2
  879.8 5.3 copy-start.9
  885.1 4.2 copy-start.25
  889.4 14.6 copy-start.23
  889.5 8.0 copy-start.16
  891.1 6.5 copy-start.35
  897.6 6.4 copy-start.18
  897.6 6.4 copy-start.37
  916.8 120.9 %reduce-scatter.7.cloned.1.call-start = ((), (), s32[]{:S(2)}) async-start(), calls=%async_computation.6 | async-start | bytes 7864320 | tf_op jit(solution)/shard_map/reduce_scatter | solution.py:162
  927.9 530.3 %all-reduce.4.cloned.1.call-start = ((), (), s32[]{:S(2)}) async-start(), calls=%async_computation.11 | async-start | bytes 25952256 | tf_op jit(solution)/shard_map/psum | solution.py:263
  927.9 12.1 copy-start.55
  927.9 22.3 %slice-start.3 = ((s8[6291456]{0:T(1024)(128)(4,1)}), s8[4194304]{0:T(1024)(128)(4,1)S(1)}, s32[]{:S(2)}) async-start(s8[6291456]{0:T(1024)(128)(4,1)} %bitcast.256), calls=%async_computation.15 | async-start | bytes 8388608
  940.0 10.3 slice-start.4
  940.0 10.3 copy-start.57
  940.0 18.9 %slice-start = ((s8[12582912]{0:T(1024)(128)(4,1)}), s8[4194304]{0:T(1024)(128)(4,1)S(1)}, s32[]{:S(2)}) async-start(s8[12582912]{0:T(1024)(128)(4,1)} %bitcast.254), calls=%async_computation.12 | async-start | bytes 8388608
  940.0 18.9 %slice-start.1 = ((s8[12582912]{0:T(1024)(128)(4,1)}), s8[4194304]{0:T(1024)(128)(4,1)S(1)}, s32[]{:S(2)}) async-start(s8[12582912]{0:T(1024)(128)(4,1)} %bitcast.254), calls=%async_computation.13 | async-start | bytes 8388608
  950.3 8.7 copy-start.19
  950.3 8.7 slice-start.2
  961.2 6.9 slice-start.5
  963.5 4.6 copy-start.13
  963.5 4.6 slice-start.6
  971.8 6.5 copy-start.47
  971.8 66.0 %copy-start.42 = (f32[1536]{0:T(1024)S(1)}, f32[1536]{0:T(1024)}, u32[]{:S(2)}) copy-start(f32[1536]{0:T(1024)} %param.25) | copy-start | bytes 18436
  971.8 66.0 %copy-start.46 = (f32[512]{0:T(512)S(1)}, f32[512]{0:T(512)}, u32[]{:S(2)}) copy-start(f32[512]{0:T(512)} %copy-done.45) | copy-start | bytes 6148
  971.8 65.9 %copy-start.49 = (f32[512]{0:T(512)S(1)}, f32[512]{0:T(512)}, u32[]{:S(2)}) copy-start(f32[512]{0:T(512)} %copy-done.48) | copy-start | bytes 6148
  1458.1 5.3 copy-start.27
  (21 other events, 56.3 us)
Sparse Core Ops, SparseCore 0:
  183.1 101.1 reduce-scatter.4
  290.4 46.3 all-gather.3
  338.4 46.3 all-gather.5
  428.5 99.0 reduce-scatter.8
  536.0 46.3 all-gather.7
  917.0 58.3 reduce-scatter.10
  978.6 59.0 reduce-scatter.6
  1044.6 413.5 all-reduce.3
